TPU v7x, 512 devices: a whole 4x8x8 slice. The times are simulated.
512 devices in a mesh: wall: 8 (over x, z_hi), row: 64 (over z_lo, y, core).
Axes of the slice: x: 4, y: 8, z: 8 (z_hi: 2, z_lo: 4; z = z_hi * 4 + z_lo), core: 2. Of those that a mesh axis runs over, the one named last changes fastest.
Arguments:
- thermal_scalars: float32 [2, 32, 1024, 1024], P(None, 'wall', 'row'), may hold values from -6 to 6
- conductive_number: float32 [2, 32], P(None, 'wall'), may hold values from 0.05 to 0.45
Outputs:
- advanced: float32 [2, 32, 1024, 1024], P(None, 'wall', 'row')
All inputs are finite; a program needn't handle non-finite values.
Results may differ from a plain program's by a relative error of at most 0.00007.
Values sent between devices are 32-bit elements; how exact they have to be, the bound alone decides.
A program may use at most 64 MiB of HBM per device.

v0:
```python
import functools
import math

import jax
import jax.numpy as jnp
import numpy as np
from jax import lax
from jax.experimental import pallas as pl
from jax.experimental.pallas import tpu as pltpu
from jax.sharding import PartitionSpec as P

STEPS = 3
MESH = pl.DeviceIdType.MESH
N = 1024
COLUMN = 16
PLANE = 32
WALLS = 8
SPECIAL = 384
HALF = math.sqrt(0.5)


def halves(table):
    table = np.asarray(table, np.float32)
    high = table.astype(jnp.bfloat16)
    low = (table - high.astype(np.float32)).astype(jnp.bfloat16)
    return np.stack([high, low])


def y_tables():
    b = np.arange(128)[None, :]
    m = np.arange(128)[:, None]
    forward, inverse = [], []
    for n in (1, 2, 3):
        angle = 2 * np.pi * ((b * (8 * m + n)) % N) / N
        c, s = np.cos(angle), np.sin(angle)
        forward.append(np.concatenate([c, s], 1))
        inverse.append(np.block([[c, s], [-s, c]]))
    m = m[:64]
    zero = 2 * np.pi * ((b * 8 * m) % N) / N
    four = 2 * np.pi * ((b * (8 * m + 4)) % N) / N
    c0, s0, c4, s4 = np.cos(zero), np.sin(zero), np.cos(four), np.sin(four)
    flip = np.where(b % 2 == 0, 1.0, -1.0)
    s0[:1] = -flip
    forward.append(np.block([[c0, s0], [c4, s4]]))
    c0[:1] *= 0.5
    s0[:1] *= 0.5
    none = np.zeros_like(c0)
    inverse.append(np.block([[c0, none], [none, c4], [-s0, none], [none, -s4]]))
    return halves(np.stack(forward)), halves(np.stack(inverse))


def x_tables():
    n = np.arange(64)
    angle = 2 * np.pi * ((n[:, None] * n[None, :]) % 64) / 64
    c, s = np.cos(angle), np.sin(angle)
    first = np.concatenate([c, s], 0)
    last = np.concatenate([c, s], 1)
    i = np.arange(16)
    small = 2 * np.pi * ((i[:, None] * i[None, :]) % 16) / 16
    c, s = np.cos(small), np.sin(small)
    into = np.zeros((2, 4, 16, 4, 2, 16))
    back = np.zeros((4, 2, 16, 2, 4, 16))
    for z in range(4):
        into[0, z, :, z, 0] = c
        into[0, z, :, z, 1] = -s
        into[1, z, :, z, 0] = s
        into[1, z, :, z, 1] = c
        back[z, 0, :, 0, z] = c
        back[z, 0, :, 1, z] = s
        back[z, 1, :, 0, z] = -s
        back[z, 1, :, 1, z] = c
    turned = np.stack([-into[1], into[0]])
    into = np.concatenate([into.reshape(128, 128), turned.reshape(128, 128)], 0)
    back_turned = np.stack([-back[:, :, :, 1], back[:, :, :, 0]], 3)
    back = np.concatenate([back.reshape(128, 128), back_turned.reshape(128, 128)], 1)
    lane = np.arange(128)
    turn = 2 * np.pi * (n[:, None] * (lane % 16)[None, :]) / N
    wave = n[:, None] + 64 * (lane % 16)[None, :]
    wave = np.where(wave > N // 2, wave - N, wave)
    square = (2 * np.pi / N * wave) ** 2
    plain = np.stack([np.cos(turn), np.sin(turn), square]).astype(np.float32)
    return halves(first), halves(last), halves(into), halves(back), plain


def split(value):
    high = value.astype(jnp.bfloat16)
    return high, (value - high.astype(jnp.float32)).astype(jnp.bfloat16)


def product(left, right, dims):
    dot = functools.partial(
        lax.dot_general, dimension_numbers=(dims, ((), ())), preferred_element_type=jnp.float32
    )
    return dot(left[0], right[0]) + (dot(left[0], right[1]) + dot(left[1], right[0]))


def pair(ref, *index):
    return ref[(0, *index)], ref[(1, *index)]


def to_waves(field, table, out, s):
    f = [field[:, 128 * a : 128 * a + 128] for a in range(8)]
    s04, d04, s26, d26 = f[0] + f[4], f[0] - f[4], f[2] + f[6], f[2] - f[6]
    s15, d15, s37, d37 = f[1] + f[5], f[1] - f[5], f[3] + f[7], f[3] - f[7]
    even, odd = s04 + s26, s15 + s37
    less, more = HALF * (d15 - d37), HALF * (d15 + d37)
    none = jnp.zeros_like(even)
    parts = [
        (d04 + less, -d26 - more),
        (s04 - s26, s37 - s15),
        (d04 - less, d26 - more),
    ]
    for j, (re, im) in enumerate(parts):
        both = jnp.concatenate(
            [jnp.concatenate([re, im], 1), jnp.concatenate([im, -re], 1)], 0
        )
        waves = product(pair(table, j), split(both), ((1,), (1,)))
        out[s, 8 * j : 8 * j + 8] = waves.reshape(8, 16, 128)
    for j, re in enumerate((even + odd, even - odd)):
        both = jnp.concatenate(
            [jnp.concatenate([re, none], 1), jnp.concatenate([none, -re], 1)], 0
        )
        rows = slice(64 * j, 64 * j + 64)
        waves = product(pair(table, 3, rows), split(both), ((1,), (1,)))
        out[s, 24 + 4 * j : 28 + 4 * j] = waves.reshape(4, 16, 128)


def from_waves(waves, table, out, s):
    u = []
    for j in range(4):
        lines = waves[s, 8 * j : 8 * j + 8].reshape(128, 128).T
        both = jnp.concatenate([lines[:64], lines[64:]], 1)
        u.append(product(split(both), pair(table, j), ((1,), (0,))))
    (re1, im1), (re2, im2), (re3, im3), (z0, z4) = [(v[:, :128], v[:, 128:]) for v in u]
    plus, minus = z0 + z4, z0 - z4
    even = [plus + re2, minus - im2, plus - re2, minus + im2]
    odd = [
        re1 + re3,
        HALF * ((re1 - im1) - (re3 + im3)),
        im3 - im1,
        HALF * ((re3 - im3) - (re1 + im1)),
    ]
    for a in range(4):
        out[s, :, :, 128 * a : 128 * a + 128] = (even[a] + odd[a]).reshape(4, 16, 128)
        out[s, :, :, 128 * a + 512 : 128 * a + 640] = (even[a] - odd[a]).reshape(4, 16, 128)


def to_spectrum(lines, first, into, plain, out, s):
    cos, sin = plain[0], plain[1]
    for w in range(WALLS):
        block = lines[s, 4 * w : 4 * w + 4].reshape(64, 128)
        both = product(pair(first), split(block), ((1,), (0,)))
        c, t = both[:64], both[64:]
        turned = jnp.concatenate([c * cos - t * sin, c * sin + t * cos], 1)
        out[s, w] = product(split(turned), pair(into), ((1,), (0,)))


def set_damping(rates, plain, square, out, s):
    q = plain[2] + square
    for w in range(WALLS):
        rate = jnp.concatenate([rates[w, s]] * 8, 0)
        out[s, w] = jnp.exp(-rate * q)


def diffuse(spectrum, rates, damping, out, s):
    lane = lax.broadcasted_iota(jnp.int32, (8, 128), 1)
    low, high = lane < 32, lane >= 96
    none = jnp.zeros((8, 128), jnp.float32)
    for block in range(8):
        rows = slice(8 * block, 8 * block + 8)
        f = [spectrum[s, w, rows] for w in range(WALLS)]
        for step in range(STEPS):
            new = []
            for w in range(WALLS):
                above = f[w + 1] if w + 1 < WALLS else none
                below = f[w - 1] if w else none
                up = pltpu.roll(jnp.where(low, above, f[w]), 96, 1)
                down = pltpu.roll(jnp.where(high, below, f[w]), 32, 1)
                curve = up + down - 2.0 * f[w]
                new.append(damping[s, w, rows] * (f[w] + rates[w, s] * curve))
            f = new
        for w in range(WALLS):
            out[w, rows] = f[w]


def from_spectrum(spectrum, back, last, plain, w):
    cos, sin = plain[0], plain[1]
    both = product(split(spectrum[w]), pair(back), ((1,), (0,)))
    value, turned = both[:, :128], both[:, 128:]
    stacked = jnp.concatenate([value * cos + turned * sin, turned * cos - value * sin], 0)
    return product(pair(last), split(stacked), ((1,), (0,)))


def kernel(
    x_ref, rate_ref, yf, yi, first, last, into, back, plain, out_ref,
    sent, middle, lines, spectrum, damped, damping, rates,
    returned, middle_back, waves, send_sem, recv_sem, rate_sem,
):
    wall, row = lax.axis_index("wall"), lax.axis_index("row")
    low, column = row // COLUMN, row % COLUMN
    plane = wall * 4 + low
    device = wall * 64 + row

    def column_peer(i):
        y, core = column // 2, column % 2
        return lax.rem(y + i // 2, 8) * 2 + lax.rem(core + i, 2)

    def plane_peer(i):
        x, z = plane // 8, plane % 8
        return lax.rem(x + i // 8, 4) * 8 + lax.rem(z + i, 8)

    def column_id(c):
        return wall, low * COLUMN + c

    def plane_id(p):
        return p // 4, lax.rem(p, 4) * COLUMN + column

    barrier = pltpu.get_barrier_semaphore()

    @pl.loop(1, PLANE)
    def _(i):
        pl.semaphore_signal(barrier, inc=1, device_id=plane_id(plane_peer(i)), device_id_type=MESH)

    @pl.loop(1, COLUMN)
    def _(i):
        pl.semaphore_signal(barrier, inc=1, device_id=column_id(column_peer(i)), device_id_type=MESH)

    def over_column(src, dst, k):
        pltpu.make_async_copy(src.at[:, column], dst.at[:, column], recv_sem.at[k]).start()

        @pl.loop(1, COLUMN)
        def _(i):
            c = column_peer(COLUMN - i)
            pltpu.make_async_remote_copy(
                src_ref=src.at[:, c], dst_ref=dst.at[:, column],
                send_sem=send_sem.at[k], recv_sem=recv_sem.at[k],
                device_id=column_id(c), device_id_type=MESH,
            ).start()

        def sent_all():
            part = pl.ds(0, COLUMN - 1)
            pltpu.make_async_copy(src.at[:, part], dst.at[:, part], send_sem.at[k]).wait()

        return lambda: pltpu.make_async_copy(src, dst, recv_sem.at[k]).wait(), sent_all

    def over_plane(src, dst, k):
        pltpu.make_async_copy(src.at[plane], dst.at[plane], recv_sem.at[k]).start()

        @pl.loop(1, PLANE)
        def _(i):
            p = plane_peer(PLANE - i)
            pltpu.make_async_remote_copy(
                src_ref=src.at[p], dst_ref=dst.at[plane],
                send_sem=send_sem.at[k], recv_sem=recv_sem.at[k],
                device_id=plane_id(p), device_id_type=MESH,
            ).start()

        def sent_all():
            part = pl.ds(0, PLANE - 1)
            pltpu.make_async_copy(src.at[part], dst.at[part], send_sem.at[k]).wait()

        return lambda: pltpu.make_async_copy(src, dst, recv_sem.at[k]).wait(), sent_all

    zone = lax.broadcasted_iota(jnp.int32, (8, 128), 1) // 32
    for s in range(2):
        value = jnp.full((8, 128), rate_ref[s, 0], jnp.float32)
        for z in range(1, 4):
            value = jnp.where(zone == z, rate_ref[s, z], value)
        rates[wall, s] = value
    to_waves(x_ref[0].reshape(64, N), yf, sent, 0)
    pl.semaphore_wait(barrier, PLANE + COLUMN - 2)
    a1, a1_sent = over_column(sent.at[0], middle.at[0], 0)
    to_waves(x_ref[1].reshape(64, N), yf, sent, 1)
    b1, b1_sent = over_plane(sent.at[1], middle.at[1], 1)

    @pl.loop(1, WALLS)
    def _(i):
        pltpu.make_async_remote_copy(
            src_ref=rates.at[wall], dst_ref=rates.at[wall],
            send_sem=rate_sem.at[0], recv_sem=rate_sem.at[1],
            device_id=(lax.rem(wall + i, WALLS), row), device_id_type=MESH,
        ).start()

    a1()
    a2, a2_sent = over_plane(middle.at[0], lines.at[0], 2)
    b1()
    b2, b2_sent = over_column(middle.at[1], lines.at[1], 3)

    group = pl.ds(0, WALLS - 1)
    pltpu.make_async_copy(rates.at[group], rates.at[group], rate_sem.at[1]).wait()
    group_of, m = device // 128, device % 128
    wave = jnp.where(group_of < 3, 8 * m + group_of + 1, 8 * lax.rem(m, 64) + 4 * (m // 64))
    wave = jnp.where(wave > N // 2, wave - N, wave)
    scale = 2.0 * math.pi / N
    scaled = scale * wave.astype(jnp.float32)
    square = scaled * scaled
    for s in range(2):
        set_damping(rates, plain, square, damping, s)

    passes = jnp.where(device == SPECIAL, 2, 1)
    part = lax.broadcasted_iota(jnp.int32, (64, 128), 1)

    def through(s):
        to_spectrum(lines, first, into, plain, spectrum, s)

        @pl.loop(0, passes)
        def _(p):
            @pl.when(p == 1)
            def _():
                set_damping(rates, plain, (scale * (N // 2)) ** 2, damping, s)

            diffuse(spectrum, rates, damping, damped, s)
            for w in range(WALLS):
                result = from_spectrum(damped, back, last, plain, w)
                at = slice(4 * w, 4 * w + 4)

                @pl.when(p == 0)
                def _():
                    returned[s, at] = result.reshape(4, 16, 128)

                @pl.when(p == 1)
                def _():
                    kept = returned[s, at].reshape(64, 128)
                    returned[s, at] = jnp.where(part < 64, kept, result).reshape(4, 16, 128)

    a2()
    through(0)
    a3, a3_sent = over_column(returned.at[0], middle_back.at[0], 4)
    b2()
    through(1)
    b3, b3_sent = over_plane(returned.at[1], middle_back.at[1], 5)
    a3()
    a4, a4_sent = over_plane(middle_back.at[0], waves.at[0], 6)
    b3()
    b4, b4_sent = over_column(middle_back.at[1], waves.at[1], 7)
    a4()
    from_waves(waves, yi, out_ref, 0)
    b4()
    from_waves(waves, yi, out_ref, 1)
    pltpu.make_async_copy(rates.at[group], rates.at[group], rate_sem.at[0]).wait()
    for done in (a1_sent, b1_sent, a2_sent, b2_sent, a3_sent, b3_sent, a4_sent, b4_sent):
        done()


def per_device(thermal_scalars, conductive_number):
    tables = [*y_tables(), *x_tables()]
    yf, yi, first, last, into, back, plain = map(jnp.asarray, tables)
    block = pltpu.VMEM((2, PLANE, COLUMN, 128), jnp.float32)
    cube = pltpu.VMEM((2, WALLS, 64, 128), jnp.float32)
    vmem = pl.BlockSpec(memory_space=pltpu.VMEM)
    result = pl.pallas_call(
        kernel,
        out_shape=jax.ShapeDtypeStruct(thermal_scalars.shape, jnp.float32),
        in_specs=[vmem, pl.BlockSpec(memory_space=pltpu.SMEM)] + [vmem] * 7,
        out_specs=vmem,
        scratch_shapes=[
            block, block, block, cube, pltpu.VMEM((WALLS, 64, 128), jnp.float32), cube,
            pltpu.VMEM((WALLS, 2, 8, 128), jnp.float32),
            block, block, block,
            pltpu.SemaphoreType.DMA((8,)), pltpu.SemaphoreType.DMA((8,)),
            pltpu.SemaphoreType.DMA((2,)),
        ],
        compiler_params=pltpu.CompilerParams(collective_id=0, has_side_effects=True),
    )(thermal_scalars, conductive_number, yf, yi, first, last, into, back, plain)
    return result * (2.0 / (N * N))


def solution(mesh):
    return jax.shard_map(
        per_device,
        mesh=mesh,
        in_specs=(P(None, "wall", "row", None), P(None, "wall")),
        out_specs=P(None, "wall", "row", None),
        check_vma=False,
    )
```

profile of v0, /device:TPU:1, one launch (start us, length us, event | category | flops | bytes accessed | tf_op | source)
XLA Modules:
  0.0 63.5 jit_solution(9129535229799638224)
XLA Ops:
  0.0 61.6 %shard_map.91 = f32[2,4,16,1024]{3,2,1,0:T(8,128)} custom-call(f32[2,4,16,1024]{3,2,1,0:T(8,128)} %x_ref.1, f32[2,4]{1,0:T(2,128)} %rate_ref.1, bf16[2,4,128,256]{3,2,1,0:T(8,128)(2,1)} %constant.16.clone.yf, bf16[2,4,256,256]{3,2,1,0:T(8,128)(2,1)} %constant.17.clone.yi, bf16[2,128,64]{2,1,0:T(8,128)(2,1)} %constant.18.clone.first, ...), custom_call_target="tpu_custom_call" | custom-call | tf_op jit(solution)/shard_map/pallas_call | solution.py:351
  61.6 1.9 %broadcast_multiply_fusion = f32[2,4,16,1024]{3,2,1,0:T(8,128)} fusion(f32[2,4,16,1024]{3,2,1,0:T(8,128)} %shard_map.91), kind=kLoop, calls=%fused_computation | loop fusion | flops 131072 | bytes 1048576 | tf_op jit(solution)/shard_map/mul | solution.py:365
where the time goes:
time: 64.3 us; the launch traced here: 63.5 us
  Pallas kernels  61.6 us (96%)
  other arithmetic  1.88 us (3%)
    pallas_call x1, Pallas kernels, per_device(): pl.pallas_call(kernel, out_shape=jax.ShapeDtypeStruct(thermal_scalars.sha...  61.6 us
    mul x1, other arithmetic, per_device(): return result * (2.0 / (N * N))  1.88 us

commit v1 on v0

v1 whole, which is shorter than its diff:
```python
import functools
import math

import jax
import jax.numpy as jnp
import numpy as np
from jax import lax
from jax.experimental import pallas as pl
from jax.experimental.pallas import tpu as pltpu
from jax.sharding import PartitionSpec as P

STEPS = 3
MESH = pl.DeviceIdType.MESH
N = 1024
COLUMN = 16
PLANE = 32
WALLS = 8
SPECIAL = 384
HALF = math.sqrt(0.5)
VMEM_LIMIT = 62 << 20


def halves(table):
    table = np.asarray(table, np.float32)
    high = table.astype(jnp.bfloat16)
    low = (table - high.astype(np.float32)).astype(jnp.bfloat16)
    return np.stack([high, low])


def y_tables():
    b = np.arange(128)[None, :]
    m = np.arange(128)[:, None]
    forward, inverse = [], []
    for n in (1, 2, 3):
        angle = 2 * np.pi * ((b * (8 * m + n)) % N) / N
        c, s = np.cos(angle), np.sin(angle)
        forward.append(np.concatenate([c, s], 1))
        inverse.append(np.block([[c, s], [-s, c]]))
    m = m[:64]
    zero = 2 * np.pi * ((b * 8 * m) % N) / N
    four = 2 * np.pi * ((b * (8 * m + 4)) % N) / N
    c0, s0, c4, s4 = np.cos(zero), np.sin(zero), np.cos(four), np.sin(four)
    flip = np.where(b % 2 == 0, 1.0, -1.0)
    s0[:1] = -flip
    forward.append(np.block([[c0, s0], [c4, s4]]))
    c0[:1] *= 0.5
    s0[:1] *= 0.5
    none = np.zeros_like(c0)
    inverse.append(np.block([[c0, none], [none, c4], [-s0, none], [none, -s4]]))
    return halves(np.stack(forward)), halves(np.stack(inverse))


def x_tables():
    n = np.arange(64)
    angle = 2 * np.pi * ((n[:, None] * n[None, :]) % 64) / 64
    c, s = np.cos(angle), np.sin(angle)
    first = np.concatenate([c, s], 0)
    last = np.concatenate([c, s], 1)
    i = np.arange(16)
    small = 2 * np.pi * ((i[:, None] * i[None, :]) % 16) / 16
    c, s = np.cos(small), np.sin(small)
    into = np.zeros((2, 2, 4, 16, 4, 2, 16))
    back = np.zeros((4, 2, 16, 2, 2, 4, 16))
    for part in range(2):
        for z in range(4):
            into[0, part, z, :, z, part] = c + s
            into[1, part, z, :, z, part] = c - s
            back[z, part, :, 0, part, z] = c + s
            back[z, part, :, 1, part, z] = c - s
    into, back = into.reshape(256, 128), back.reshape(128, 256)
    lane = np.arange(128)
    turn = 2 * np.pi * (n[:, None] * (lane % 16)[None, :]) / N
    wave = n[:, None] + 64 * (lane % 16)[None, :]
    wave = np.where(wave > N // 2, wave - N, wave)
    square = (2 * np.pi / N * wave) ** 2
    plain = np.stack([np.cos(turn), np.sin(turn), square]).astype(np.float32)
    return halves(first), halves(last), halves(into), halves(back), plain


def split(value):
    high = value.astype(jnp.bfloat16)
    return high, (value - high.astype(jnp.float32)).astype(jnp.bfloat16)


def product(left, right, dims):
    dot = functools.partial(
        lax.dot_general, dimension_numbers=(dims, ((), ())), preferred_element_type=jnp.float32
    )
    return dot(left[0], right[0]) + (dot(left[0], right[1]) + dot(left[1], right[0]))


def pair(ref, *index):
    return ref[(0, *index)], ref[(1, *index)]


def to_waves(field, table, out, s):
    f = [field[:, 128 * a : 128 * a + 128] for a in range(8)]
    s04, d04, s26, d26 = f[0] + f[4], f[0] - f[4], f[2] + f[6], f[2] - f[6]
    s15, d15, s37, d37 = f[1] + f[5], f[1] - f[5], f[3] + f[7], f[3] - f[7]
    even, odd = s04 + s26, s15 + s37
    less, more = HALF * (d15 - d37), HALF * (d15 + d37)
    none = jnp.zeros_like(even)
    parts = [
        (d04 + less, -d26 - more),
        (s04 - s26, s37 - s15),
        (d04 - less, d26 - more),
    ]
    for j, (re, im) in enumerate(parts):
        both = jnp.concatenate(
            [jnp.concatenate([re, im], 1), jnp.concatenate([im, -re], 1)], 0
        )
        waves = product(pair(table, j), split(both), ((1,), (1,)))
        out[s, 8 * j : 8 * j + 8] = waves.reshape(8, 16, 128)
    for j, re in enumerate((even + odd, even - odd)):
        both = jnp.concatenate(
            [jnp.concatenate([re, none], 1), jnp.concatenate([none, -re], 1)], 0
        )
        rows = slice(64 * j, 64 * j + 64)
        waves = product(pair(table, 3, rows), split(both), ((1,), (1,)))
        out[s, 24 + 4 * j : 28 + 4 * j] = waves.reshape(4, 16, 128)


def from_waves(waves, table, out, s):
    u = []
    for j in range(4):
        lines = waves[s, 8 * j : 8 * j + 8].reshape(128, 128).T
        both = jnp.concatenate([lines[:64], lines[64:]], 1)
        u.append(product(split(both), pair(table, j), ((1,), (0,))))
    (re1, im1), (re2, im2), (re3, im3), (z0, z4) = [(v[:, :128], v[:, 128:]) for v in u]
    plus, minus = z0 + z4, z0 - z4
    even = [plus + re2, minus - im2, plus - re2, minus + im2]
    odd = [
        re1 + re3,
        HALF * ((re1 - im1) - (re3 + im3)),
        im3 - im1,
        HALF * ((re3 - im3) - (re1 + im1)),
    ]
    for a in range(4):
        out[s, :, :, 128 * a : 128 * a + 128] = (even[a] + odd[a]).reshape(4, 16, 128)
        out[s, :, :, 128 * a + 512 : 128 * a + 640] = (even[a] - odd[a]).reshape(4, 16, 128)


def to_spectrum(lines, first, into, plain, out, s, w):
    cos, sin = plain[0], plain[1]
    block = lines[s, pl.ds(4 * w, 4)].reshape(64, 128)
    both = product(pair(first), split(block), ((1,), (0,)))
    c, t = both[:64], both[64:]
    turned = jnp.concatenate([c * cos - t * sin, c * sin + t * cos], 1)
    out[s, w] = product(split(turned), pair(into), ((1,), (0,)))


def set_damping(rates, plain, square, out, s):
    q = plain[2] + square
    for w in range(WALLS):
        rate = jnp.concatenate([rates[w, s]] * 8, 0)
        out[s, w] = jnp.exp(-rate * q)


def diffuse(spectrum, rates, damping, out, s):
    lane = lax.broadcasted_iota(jnp.int32, (8, 128), 1)
    low, high = lane < 32, lane >= 96
    none = jnp.zeros((8, 128), jnp.float32)
    for block in range(8):
        rows = slice(8 * block, 8 * block + 8)
        f = [spectrum[s, w, rows] for w in range(WALLS)]
        for step in range(STEPS):
            new = []
            for w in range(WALLS):
                above = f[w + 1] if w + 1 < WALLS else none
                below = f[w - 1] if w else none
                up = pltpu.roll(jnp.where(low, above, f[w]), 96, 1)
                down = pltpu.roll(jnp.where(high, below, f[w]), 32, 1)
                curve = up + down - 2.0 * f[w]
                new.append(damping[s, w, rows] * (f[w] + rates[w, s] * curve))
            f = new
        for w in range(WALLS):
            out[w, rows] = f[w]


def from_spectrum(spectrum, back, last, plain, w):
    cos, sin = plain[0], plain[1]
    both = product(split(spectrum[w]), pair(back), ((1,), (0,)))
    value, turned = both[:, :128], both[:, 128:]
    stacked = jnp.concatenate([value * cos + turned * sin, turned * cos - value * sin], 0)
    return product(pair(last), split(stacked), ((1,), (0,)))


def kernel(
    x_hbm, rate_ref, yf_hbm, yi_hbm, first_hbm, last_hbm, into_hbm, back_hbm, plain_hbm, out_ref,
    x_ref, yf, yi, first, last, into, back, plain,
    sent, middle, lines, spectrum, damped, damping, rates,
    returned, middle_back, waves, load_sem, send_sem, recv_sem, rate_sem,
):
    wall, row = lax.axis_index("wall"), lax.axis_index("row")
    low, column = row // COLUMN, row % COLUMN
    plane = wall * 4 + low
    device = wall * 64 + row
    x, z, y, core = plane // 8, plane % 8, column // 2, column % 2

    loads = [
        (x_hbm.at[0], x_ref.at[0]), (yf_hbm, yf), (x_hbm.at[1], x_ref.at[1]), (plain_hbm, plain),
        (first_hbm, first), (into_hbm, into), (back_hbm, back), (last_hbm, last), (yi_hbm, yi),
    ]
    loads = [pltpu.make_async_copy(*refs, load_sem.at[k]) for k, refs in enumerate(loads)]
    for load in loads[:3]:
        load.start()

    def column_id(c):
        return wall, low * COLUMN + c

    def plane_id(p):
        return p // 4, lax.rem(p, 4) * COLUMN + column

    def column_peer(h, i):
        half = (y // 4 + 1 - h) % 2
        return (half * 4 + (y + i // 2) % 4) * 2 + (core + i) % 2

    def plane_peer(h, i):
        half = (x // 2 + 1 - h) % 2
        return (half * 2 + (x + i // 8) % 2) * 8 + (z + i) % 8

    barrier = pltpu.get_barrier_semaphore()
    for h in range(2):

        @pl.loop(h, 16)
        def _(i):
            to = plane_id(plane_peer(h, i))
            pl.semaphore_signal(barrier, inc=1, device_id=to, device_id_type=MESH)

        @pl.loop(h, 8)
        def _(i):
            to = column_id(column_peer(h, i))
            pl.semaphore_signal(barrier, inc=1, device_id=to, device_id_type=MESH)

    for load in loads[3:]:
        load.start()

    whole_x, whole_y = pl.ds(0, PLANE), pl.ds(0, COLUMN)
    half_x = [pl.ds(pl.multiple_of((x // 2 + 1 - h) % 2 * 16, 16), 16) for h in range(2)]
    half_y = [pl.ds(pl.multiple_of((y // 4 + 1 - h) % 2 * 8, 8), 8) for h in range(2)]
    done = []

    def remote(src, dst, k, to):
        pltpu.make_async_remote_copy(
            src_ref=src, dst_ref=dst, send_sem=send_sem.at[k], recv_sem=recv_sem.at[k],
            device_id=to, device_id_type=MESH,
        ).start()

    def await_block(src, dst, sem, rows, columns):
        part = (pl.ds(0, rows), pl.ds(0, columns))
        return pltpu.make_async_copy(src.at[part], dst.at[part], sem).wait

    def over_column(src, dst, k, xs, n, halves):
        if 1 in halves:
            pltpu.make_async_copy(src.at[xs, column], dst.at[xs, column], recv_sem.at[k]).start()
        for h in halves:

            @pl.loop(h, 8)
            def _(i):
                c = column_peer(h, i)
                remote(src.at[xs, c], dst.at[xs, column], k, column_id(c))

        count = 8 * len(halves)
        done.append(await_block(src, dst, send_sem.at[k], n, count - (1 in halves)))
        return await_block(src, dst, recv_sem.at[k], n, count)

    def to_planes(src, dst, k, ys, h):
        if h:
            pltpu.make_async_copy(src.at[plane, ys], dst.at[plane, ys], recv_sem.at[k]).start()

        @pl.loop(h, 16)
        def _(i):
            p = plane_peer(h, i)
            remote(src.at[p, ys], dst.at[plane, ys], k, plane_id(p))

    def over_plane(src, dst, k, ys, n, halves):
        for h in halves:
            to_planes(src, dst, k, ys, h)
        count = 16 * len(halves)
        done.append(await_block(src, dst, send_sem.at[k], count - (1 in halves), n))
        return await_block(src, dst, recv_sem.at[k], count, n)

    zone = lax.broadcasted_iota(jnp.int32, (8, 128), 1) // 32
    for s in range(2):
        value = jnp.full((8, 128), rate_ref[s, 0], jnp.float32)
        for j in range(1, 4):
            value = jnp.where(zone == j, rate_ref[s, j], value)
        rates[wall, s] = value
    for s in range(2):
        if s == 0:
            loads[1].wait()
        loads[2 * s].wait()
        to_waves(x_ref[s].reshape(64, N), yf, sent, s)
    pl.semaphore_wait(barrier, PLANE + COLUMN - 2)

    both = (0, 1)
    a1, b1, a2, b2 = [], [], [], []
    for h in both:
        a1.append(over_column(sent.at[0], middle.at[0], h, half_x[h], 16, both))
        b1.append(over_plane(sent.at[1], middle.at[1], 2 + h, half_y[h], 8, both))

    @pl.loop(1, WALLS)
    def _(i):
        pltpu.make_async_remote_copy(
            src_ref=rates.at[wall], dst_ref=rates.at[wall],
            send_sem=rate_sem.at[0], recv_sem=rate_sem.at[1],
            device_id=(lax.rem(wall + i, WALLS), row), device_id_type=MESH,
        ).start()

    for h in both:
        a1[h]()
        a2.append(over_plane(middle.at[0], lines.at[0], 4 + h, whole_y, COLUMN, (h,)))
        b1[h]()
        b2.append(over_column(middle.at[1], lines.at[1], 6 + h, whole_x, PLANE, (h,)))

    group = pl.ds(0, WALLS - 1)
    pltpu.make_async_copy(rates.at[group], rates.at[group], rate_sem.at[1]).wait()
    for load in loads[3:]:
        load.wait()
    group_of, m = device // 128, device % 128
    wave = jnp.where(group_of < 3, 8 * m + group_of + 1, 8 * lax.rem(m, 64) + 4 * (m // 64))
    wave = jnp.where(wave > N // 2, wave - N, wave)
    other = jnp.where(device == SPECIAL, N // 2, wave)
    scale = 2.0 * math.pi / N
    scaled, scaled_other = scale * wave.astype(jnp.float32), scale * other.astype(jnp.float32)
    part = lax.broadcasted_iota(jnp.int32, (64, 128), 1) // 16 % 2
    square = jnp.where(part == 0, scaled * scaled, scaled_other * scaled_other)
    for s in both:
        set_damping(rates, plain, square, damping, s)

    slabs = [[(x // 2 + 1 - h) % 2 * 4 + j for j in range(4)] for h in both]

    def back_to_lines(s, h):
        for w in slabs[h]:
            lines_back = from_spectrum(damped, back, last, plain, w)
            returned[s, pl.ds(4 * w, 4)] = lines_back.reshape(4, 16, 128)

    for h in both:
        a2[h]()
        for w in slabs[h]:
            to_spectrum(lines, first, into, plain, spectrum, 0, w)
    diffuse(spectrum, rates, damping, damped, 0)
    a3, b3, a4, b4 = [], [], [], []
    for h in both:
        back_to_lines(0, h)
        a3.append(over_column(returned.at[0], middle_back.at[0], 8 + h, half_x[h], 16, both))
    for h in both:
        b2[h]()
    for w in range(WALLS):
        to_spectrum(lines, first, into, plain, spectrum, 1, w)
    diffuse(spectrum, rates, damping, damped, 1)
    for h in both:
        back_to_lines(1, h)
        for half in both:
            to_planes(returned.at[1], middle_back.at[1], 10 + half, half_y[half], h)
    for h in both:
        src, dst = returned.at[1], middle_back.at[1]
        done.append(await_block(src, dst, send_sem.at[10 + h], PLANE - 1, 8))
        b3.append(await_block(src, dst, recv_sem.at[10 + h], PLANE, 8))
    for h in both:
        a3[h]()
        a4.append(over_plane(middle_back.at[0], waves.at[0], 12 + h, whole_y, COLUMN, (h,)))
        b3[h]()
        b4.append(over_column(middle_back.at[1], waves.at[1], 14 + h, whole_x, PLANE, (h,)))
    for h in both:
        a4[h]()
    from_waves(waves, yi, out_ref, 0)
    for h in both:
        b4[h]()
    from_waves(waves, yi, out_ref, 1)
    pltpu.make_async_copy(rates.at[group], rates.at[group], rate_sem.at[0]).wait()
    for wait in done:
        wait()


def per_device(thermal_scalars, conductive_number):
    tables = [*y_tables(), *x_tables()]
    arrays = [jnp.asarray(t) for t in tables]
    block = pltpu.VMEM((2, PLANE, COLUMN, 128), jnp.float32)
    cube = pltpu.VMEM((2, WALLS, 64, 128), jnp.float32)
    far = pl.BlockSpec(memory_space=pltpu.HBM)
    loaded = [pltpu.VMEM(v.shape, v.dtype) for v in (thermal_scalars, *arrays)]
    result = pl.pallas_call(
        kernel,
        out_shape=jax.ShapeDtypeStruct(thermal_scalars.shape, jnp.float32),
        in_specs=[far, pl.BlockSpec(memory_space=pltpu.SMEM)] + [far] * 7,
        out_specs=pl.BlockSpec(memory_space=pltpu.VMEM),
        scratch_shapes=[
            *loaded,
            block, block, block, cube, pltpu.VMEM((WALLS, 64, 128), jnp.float32), cube,
            pltpu.VMEM((WALLS, 2, 8, 128), jnp.float32),
            block, block, block,
            pltpu.SemaphoreType.DMA((9,)), pltpu.SemaphoreType.DMA((16,)),
            pltpu.SemaphoreType.DMA((16,)), pltpu.SemaphoreType.DMA((2,)),
        ],
        compiler_params=pltpu.CompilerParams(
            collective_id=0, has_side_effects=True, vmem_limit_bytes=VMEM_LIMIT
        ),
    )(thermal_scalars, conductive_number, *arrays)
    return result * (2.0 / (N * N))


def solution(mesh):
    return jax.shard_map(
        per_device,
        mesh=mesh,
        in_specs=(P(None, "wall", "row", None), P(None, "wall")),
        out_specs=P(None, "wall", "row", None),
        check_vma=False,
    )
```

time: 64.3 us -> 56.3 us (0.88); the launches traced: 63.5 us -> 56.1 us
  Pallas kernels: 61.6 us -> 54.3 us
    pallas_call x1, Pallas kernels: 61.6 us -> 54.3 us  [per_device(): pl.pallas_call(kernel, out_shape=jax.ShapeDtypeStruct(thermal_scalars.sha...]
where the time goes in v1:
time: 56.3 us; the launch traced here: 56.1 us
  Pallas kernels  54.3 us (96%)
  other arithmetic  1.88 us (3%)
    pallas_call x1, Pallas kernels, per_device(): pl.pallas_call(kernel, out_shape=jax.ShapeDtypeStruct(thermal_scalars.sha...  54.3 us
    mul x1, other arithmetic, per_device(): return result * (2.0 / (N * N))  1.88 us

profile of v1, /device:TPU:1, one launch (start us, length us, event | category | flops | bytes accessed | tf_op | source)
XLA Modules:
  0.0 56.1 jit_solution(9606553036325626697)
XLA Ops:
  0.0 54.3 %shard_map.91 = f32[2,4,16,1024]{3,2,1,0:T(8,128)} custom-call(f32[2,4,16,1024]{3,2,1,0:T(8,128)} %x_hbm.1, f32[2,4]{1,0:T(2,128)} %rate_ref.1, bf16[2,4,128,256]{3,2,1,0:T(8,128)(2,1)} %constant.16.clone.yf_hbm, bf16[2,4,256,256]{3,2,1,0:T(8,128)(2,1)} %constant.17.clone.yi_hbm, bf16[2,128,64]{2,1,0:T(8,128)(2,1)} %constant.18.clone.first_hbm, ...), custom_call_target="tpu_custom_call" | custom-call | tf_op jit(solution)/shard_map/pallas_call | solution.py:383
  54.3 1.9 %broadcast_multiply_fusion = f32[2,4,16,1024]{3,2,1,0:T(8,128)} fusion(f32[2,4,16,1024]{3,2,1,0:T(8,128)} %shard_map.91), kind=kLoop, calls=%fused_computation | loop fusion | flops 131072 | bytes 1048576 | tf_op jit(solution)/shard_map/mul | solution.py:400

commit v2 on v1

v2 whole, which is shorter than its diff:
```python
import functools
import math

import jax
import jax.numpy as jnp
import numpy as np
from jax import lax
from jax.experimental import pallas as pl
from jax.experimental.pallas import tpu as pltpu
from jax.sharding import PartitionSpec as P

STEPS = 3
MESH = pl.DeviceIdType.MESH
N = 1024
COLUMN = 16
PLANE = 32
WALLS = 8
SPECIAL = 384
HALF = math.sqrt(0.5)
VMEM_LIMIT = 54400 << 10


def halves(table):
    table = np.asarray(table, np.float32)
    high = table.astype(jnp.bfloat16)
    low = (table - high.astype(np.float32)).astype(jnp.bfloat16)
    return np.stack([high, low])


def y_tables():
    b = np.arange(128)[None, :]
    m = np.arange(128)[:, None]
    forward, inverse = [], []
    for n in (1, 2, 3):
        angle = 2 * np.pi * ((b * (8 * m + n)) % N) / N
        c, s = np.cos(angle), np.sin(angle)
        forward.append(np.concatenate([c, s], 1))
        inverse.append(np.block([[c, s], [-s, c]]))
    m = m[:64]
    zero = 2 * np.pi * ((b * 8 * m) % N) / N
    four = 2 * np.pi * ((b * (8 * m + 4)) % N) / N
    c0, s0, c4, s4 = np.cos(zero), np.sin(zero), np.cos(four), np.sin(four)
    flip = np.where(b % 2 == 0, 1.0, -1.0)
    s0[:1] = -flip
    forward.append(np.block([[c0, s0], [c4, s4]]))
    c0[:1] *= 0.5
    s0[:1] *= 0.5
    none = np.zeros_like(c0)
    inverse.append(np.block([[c0, none], [none, c4], [-s0, none], [none, -s4]]))
    return np.stack(forward), np.stack(inverse)


def x_tables():
    n = np.arange(64)
    angle = 2 * np.pi * ((n[:, None] * n[None, :]) % 64) / 64
    c, s = np.cos(angle), np.sin(angle)
    first = np.concatenate([c, s], 0)
    last = np.concatenate([c, s], 1)
    i = np.arange(16)
    small = 2 * np.pi * ((i[:, None] * i[None, :]) % 16) / 16
    c, s = np.cos(small), np.sin(small)
    into = np.zeros((2, 2, 4, 16, 4, 2, 16))
    back = np.zeros((4, 2, 16, 2, 2, 4, 16))
    for part in range(2):
        for z in range(4):
            into[0, part, z, :, z, part] = c + s
            into[1, part, z, :, z, part] = c - s
            back[z, part, :, 0, part, z] = c + s
            back[z, part, :, 1, part, z] = c - s
    into, back = into.reshape(256, 128), back.reshape(128, 256)
    lane = np.arange(128)
    turn = 2 * np.pi * (n[:, None] * (lane % 16)[None, :]) / N
    return first, last, into, back, np.cos(turn), np.sin(turn)


def packed_tables():
    forward, inverse = y_tables()
    first, last, into, back, cos, sin = x_tables()
    packed = np.zeros((2, 1664, 256), jnp.bfloat16)
    packed[:, :1024] = halves(inverse.reshape(1024, 256))
    for table, place in ((back, BACK), (into, INTO), (last, LAST), (first, FIRST)):
        packed[(slice(None), *place)] = halves(table)
    for j, table in enumerate((cos, sin)):
        rest = table.astype(np.float32)
        for i in range(3):
            term = rest.astype(jnp.bfloat16)
            packed[(j, *turn_place(i))] = term
            rest = rest - term.astype(np.float32)
    return halves(forward), packed


def turn_place(i):
    return slice(1408 + 64 * i, 1472 + 64 * i), slice(0, 128)


BACK = slice(1024, 1152), slice(0, 256)
INTO = slice(1152, 1408), slice(0, 128)
LAST = slice(1152, 1216), slice(128, 256)
FIRST = slice(1216, 1344), slice(128, 192)


def split(value):
    high = value.astype(jnp.bfloat16)
    return high, (value - high.astype(jnp.float32)).astype(jnp.bfloat16)


def product(left, right, dims):
    dot = functools.partial(
        lax.dot_general, dimension_numbers=(dims, ((), ())), preferred_element_type=jnp.float32
    )
    return dot(left[0], right[0]) + (dot(left[0], right[1]) + dot(left[1], right[0]))


def pair(ref, *index):
    return ref[(0, *index)], ref[(1, *index)]


def to_waves(field, table, out, s):
    f = [field[:, 128 * a : 128 * a + 128] for a in range(8)]
    s04, d04, s26, d26 = f[0] + f[4], f[0] - f[4], f[2] + f[6], f[2] - f[6]
    s15, d15, s37, d37 = f[1] + f[5], f[1] - f[5], f[3] + f[7], f[3] - f[7]
    even, odd = s04 + s26, s15 + s37
    less, more = HALF * (d15 - d37), HALF * (d15 + d37)
    none = jnp.zeros_like(even)
    parts = [
        (d04 + less, -d26 - more),
        (s04 - s26, s37 - s15),
        (d04 - less, d26 - more),
    ]
    for j, (re, im) in enumerate(parts):
        both = jnp.concatenate(
            [jnp.concatenate([re, im], 1), jnp.concatenate([im, -re], 1)], 0
        )
        waves = product(pair(table, j), split(both), ((1,), (1,)))
        out[s, 8 * j : 8 * j + 8] = waves.reshape(8, 16, 128)
    for j, re in enumerate((even + odd, even - odd)):
        both = jnp.concatenate(
            [jnp.concatenate([re, none], 1), jnp.concatenate([none, -re], 1)], 0
        )
        rows = slice(64 * j, 64 * j + 64)
        waves = product(pair(table, 3, rows), split(both), ((1,), (1,)))
        out[s, 24 + 4 * j : 28 + 4 * j] = waves.reshape(4, 16, 128)


def from_waves(waves, table, out, s):
    u = []
    for j in range(4):
        lines = waves[s, 8 * j : 8 * j + 8].reshape(128, 128).T
        both = jnp.concatenate([lines[:64], lines[64:]], 1)
        u.append(product(split(both), pair(table, slice(256 * j, 256 * j + 256)), ((1,), (0,))))
    (re1, im1), (re2, im2), (re3, im3), (z0, z4) = [(v[:, :128], v[:, 128:]) for v in u]
    plus, minus = z0 + z4, z0 - z4
    even = [plus + re2, minus - im2, plus - re2, minus + im2]
    odd = [
        re1 + re3,
        HALF * ((re1 - im1) - (re3 + im3)),
        im3 - im1,
        HALF * ((re3 - im3) - (re1 + im1)),
    ]
    for a in range(4):
        out[s, :, :, 128 * a : 128 * a + 128] = (even[a] + odd[a]).reshape(4, 16, 128)
        out[s, :, :, 128 * a + 512 : 128 * a + 640] = (even[a] - odd[a]).reshape(4, 16, 128)


def to_spectrum(lines, tables, plain, out, s, w):
    cos, sin = plain[0], plain[1]
    block = lines[s, pl.ds(4 * w, 4)].reshape(64, 128)
    both = product(pair(tables, *FIRST), split(block), ((1,), (0,)))
    c, t = both[:64], both[64:]
    turned = jnp.concatenate([c * cos - t * sin, c * sin + t * cos], 1)
    out[s, w] = product(split(turned), pair(tables, *INTO), ((1,), (0,)))


def set_damping(rates, square, out, s):
    for w in range(WALLS):
        rate = jnp.concatenate([rates[w, s]] * 8, 0)
        out[s, w] = jnp.exp(-rate * square)


def diffuse(spectrum, rates, damping, out, s):
    lane = lax.broadcasted_iota(jnp.int32, (64, 128), 1)
    low, high = lane < 32, lane >= 96
    none = jnp.zeros((64, 128), jnp.float32)
    f = [spectrum[s, w] for w in range(WALLS)]
    for step in range(STEPS):
        new = []
        for w in range(WALLS):
            above = f[w + 1] if w + 1 < WALLS else none
            below = f[w - 1] if w else none
            up = pltpu.roll(jnp.where(low, above, f[w]), 96, 1)
            down = pltpu.roll(jnp.where(high, below, f[w]), 32, 1)
            rate = jnp.concatenate([rates[w, s]] * 8, 0)
            new.append(damping[s, w] * (f[w] + rate * (up + down - 2.0 * f[w])))
        f = new
    for w in range(WALLS):
        out[w] = f[w]


def from_spectrum(spectrum, tables, plain, w):
    cos, sin = plain[0], plain[1]
    both = product(split(spectrum[w]), pair(tables, *BACK), ((1,), (0,)))
    value, turned = both[:, :128], both[:, 128:]
    stacked = jnp.concatenate([value * cos + turned * sin, turned * cos - value * sin], 0)
    return product(pair(tables, *LAST), split(stacked), ((1,), (0,)))


def kernel(
    x_hbm, rate_ref, yf_hbm, tables_hbm, out_ref, x_ref, yf, tables, plain,
    sent, middle, lines, spectrum, damped, damping, rates,
    returned, middle_back, waves, load_sem, send_sem, recv_sem, rate_sem,
):
    wall, row = lax.axis_index("wall"), lax.axis_index("row")
    low, column = row // COLUMN, row % COLUMN
    plane = wall * 4 + low
    device = wall * 64 + row
    x, z, y, core = plane // 8, plane % 8, column // 2, column % 2

    loads = [
        (x_hbm.at[0], x_ref.at[0]), (yf_hbm, yf), (x_hbm.at[1], x_ref.at[1]), (tables_hbm, tables),
    ]
    loads = [pltpu.make_async_copy(*refs, load_sem.at[k]) for k, refs in enumerate(loads)]
    for load in loads[:3]:
        load.start()

    def column_id(c):
        return wall, low * COLUMN + c

    def plane_id(p):
        return p // 4, lax.rem(p, 4) * COLUMN + column

    def column_peer(h, i):
        half = (y // 4 + 1 - h) % 2
        return (half * 4 + (y + i // 2) % 4) * 2 + (core + i) % 2

    far_x = [(x // 2 + 1) % 2 * 2 + (x + q) % 2 for q in range(2)]

    def far_peer(q, i):
        return far_x[q] * 8 + (z + i) % 8

    def near_peer(i):
        return (x // 2 * 2 + (x + i // 8) % 2) * 8 + (z + i) % 8

    barrier = pltpu.get_barrier_semaphore()

    def greet(to):
        pl.semaphore_signal(barrier, inc=1, device_id=to, device_id_type=MESH)

    for q in range(2):
        for i in (4, 3, 5, 2, 6, 1, 7, 0):
            greet(plane_id(far_peer(q, i)))
    for i in range(8):
        greet(column_id(column_peer(0, i)))
    for i in range(15, 0, -1):
        greet(plane_id(near_peer(i)))
    for i in range(1, 8):
        greet(column_id(column_peer(1, i)))

    loads[3].start()

    half_x = [pl.ds(pl.multiple_of((x // 2 + 1 - h) % 2 * 16, 16), 16) for h in range(2)]
    quarter_x = [pl.ds(pl.multiple_of(far_x[q] * 8, 8), 8) for q in range(2)]
    half_y = [pl.ds(pl.multiple_of((y // 4 + 1 - h) % 2 * 8, 8), 8) for h in range(2)]
    done = []

    def remote(src, dst, k, to):
        pltpu.make_async_remote_copy(
            src_ref=src, dst_ref=dst, send_sem=send_sem.at[k], recv_sem=recv_sem.at[k],
            device_id=to, device_id_type=MESH,
        ).start()

    def await_block(src, dst, sem, rows, columns):
        part = (pl.ds(0, rows), pl.ds(0, columns))
        return pltpu.make_async_copy(src.at[part], dst.at[part], sem).wait

    def to_column(src, dst, k, xs, h):
        if h:
            pltpu.make_async_copy(src.at[xs, column], dst.at[xs, column], recv_sem.at[k]).start()

        @pl.loop(h, 8)
        def _(i):
            c = column_peer(h, i)
            remote(src.at[xs, c], dst.at[xs, column], k, column_id(c))

    def expect(src, dst, k, rows, columns, out_rows, out_columns):
        done.append(await_block(src, dst, send_sem.at[k], out_rows, out_columns))
        return await_block(src, dst, recv_sem.at[k], rows, columns)

    def far_first(src, mid, k, q):
        for h in range(2):
            to_column(src, mid, k + q, quarter_x[q], h)
        return expect(src, mid, k + q, 8, 16, 8, 15)

    def far_second(mid, dst, k, q):
        @pl.loop(0, 8)
        def _(i):
            p = far_peer(q, i)
            remote(mid.at[p], dst.at[plane], k + 2, plane_id(p))

        return expect(mid, dst, k + 2, 16, 16, 16, 16) if q else None

    def near_first(src, mid, k, q):
        ys = half_y[q]
        pltpu.make_async_copy(
            src.at[plane, ys], mid.at[plane, ys], recv_sem.at[k + 3 + q]
        ).start()

        @pl.loop(1, 16)
        def _(i):
            p = near_peer(i)
            remote(src.at[p, ys], mid.at[plane, ys], k + 3 + q, plane_id(p))

        return expect(src, mid, k + 3 + q, 16, 8, 15, 8)

    def near_second(mid, dst, k, q):
        to_column(mid, dst, k + 5, half_x[1], q)
        return expect(mid, dst, k + 5, 16, 16, 16, 15) if q else None

    zone = lax.broadcasted_iota(jnp.int32, (8, 128), 1) // 32
    for s in range(2):
        value = jnp.full((8, 128), rate_ref[s, 0], jnp.float32)
        for j in range(1, 4):
            value = jnp.where(zone == j, rate_ref[s, j], value)
        rates[wall, s] = value
    for s in range(2):
        if s == 0:
            loads[1].wait()
        loads[2 * s].wait()
        to_waves(x_ref[s].reshape(64, N), yf, sent, s)
    pl.semaphore_wait(barrier, PLANE + COLUMN - 2)

    both = (0, 1)
    first_steps = []
    for s in both:
        for q in both:
            first_steps.append(far_first(sent.at[s], middle.at[s], 6 * s, q))
            first_steps.append(near_first(sent.at[s], middle.at[s], 6 * s, q))

    @pl.loop(1, WALLS)
    def _(i):
        pltpu.make_async_remote_copy(
            src_ref=rates.at[wall], dst_ref=rates.at[wall],
            send_sem=rate_sem.at[0], recv_sem=rate_sem.at[1],
            device_id=(lax.rem(wall + i, WALLS), row), device_id_type=MESH,
        ).start()

    def second_steps(waits, mid, dst, k):
        for q in both:
            waits[2 * q]()
            far = far_second(mid, dst, k, q)
            waits[2 * q + 1]()
            near = near_second(mid, dst, k, q)
        return far, near

    arrived = [
        second_steps(first_steps[4 * s : 4 * s + 4], middle.at[s], lines.at[s], 6 * s)
        for s in both
    ]

    group = pl.ds(0, WALLS - 1)
    pltpu.make_async_copy(rates.at[group], rates.at[group], rate_sem.at[1]).wait()
    loads[3].wait()
    for j in range(2):
        terms = [tables[(j, *turn_place(i))].astype(jnp.float32) for i in range(3)]
        plain[j] = terms[0] + (terms[1] + terms[2])
    group_of, m = device // 128, device % 128
    wave = jnp.where(group_of < 3, 8 * m + group_of + 1, 8 * lax.rem(m, 64) + 4 * (m // 64))
    wave = jnp.where(wave > N // 2, wave - N, wave)
    other = jnp.where(device == SPECIAL, N // 2, wave)
    scale = 2.0 * math.pi / N
    scaled, scaled_other = scale * wave.astype(jnp.float32), scale * other.astype(jnp.float32)
    lane = lax.broadcasted_iota(jnp.int32, (64, 128), 1)
    square = jnp.where(lane // 16 % 2 == 0, scaled * scaled, scaled_other * scaled_other)
    wave_x = lax.broadcasted_iota(jnp.int32, (64, 128), 0) + 64 * (lane % 16)
    wave_x = scale * jnp.where(wave_x > N // 2, wave_x - N, wave_x).astype(jnp.float32)
    square = square + wave_x * wave_x
    for s in both:
        set_damping(rates, square, damping, s)

    slabs = [[(x // 2 + 1 - h) % 2 * 4 + j for j in range(4)] for h in both]

    def back_to_lines(s, h):
        for w in slabs[h]:
            lines_back = from_spectrum(damped, tables, plain, w)
            returned[s, pl.ds(4 * w, 4)] = lines_back.reshape(4, 16, 128)

    first_steps = []
    for s in both:
        for h in both:
            arrived[s][h]()
            for w in slabs[h]:
                to_spectrum(lines, tables, plain, spectrum, s, w)
        diffuse(spectrum, rates, damping, damped, s)
        for h, send in enumerate((far_first, near_first)):
            back_to_lines(s, h)
            for q in both:
                first_steps.append(send(returned.at[s], middle_back.at[s], 12 + 6 * s, q))
    for s in both:
        far0, far1, near0, near1 = first_steps[4 * s : 4 * s + 4]
        waits = far0, near0, far1, near1
        arrived[s] = second_steps(waits, middle_back.at[s], waves.at[s], 12 + 6 * s)
    for s in both:
        for wait in arrived[s]:
            wait()
        from_waves(waves, tables, out_ref, s)
    pltpu.make_async_copy(rates.at[group], rates.at[group], rate_sem.at[0]).wait()
    for wait in done:
        wait()


def per_device(thermal_scalars, conductive_number):
    arrays = [jnp.asarray(table) for table in packed_tables()]
    block = pltpu.VMEM((2, PLANE, COLUMN, 128), jnp.float32)
    cube = pltpu.VMEM((2, WALLS, 64, 128), jnp.float32)
    far = pl.BlockSpec(memory_space=pltpu.HBM)
    loaded = [pltpu.VMEM(v.shape, v.dtype) for v in (thermal_scalars, *arrays)]
    result = pl.pallas_call(
        kernel,
        out_shape=jax.ShapeDtypeStruct(thermal_scalars.shape, jnp.float32),
        in_specs=[far, pl.BlockSpec(memory_space=pltpu.SMEM)] + [far] * 2,
        out_specs=pl.BlockSpec(memory_space=pltpu.VMEM),
        scratch_shapes=[
            *loaded, pltpu.VMEM((2, 64, 128), jnp.float32),
            block, block, block, cube, pltpu.VMEM((WALLS, 64, 128), jnp.float32), cube,
            pltpu.VMEM((WALLS, 2, 8, 128), jnp.float32),
            block, block, block,
            pltpu.SemaphoreType.DMA((4,)), pltpu.SemaphoreType.DMA((24,)),
            pltpu.SemaphoreType.DMA((24,)), pltpu.SemaphoreType.DMA((2,)),
        ],
        compiler_params=pltpu.CompilerParams(
            collective_id=0, has_side_effects=True, vmem_limit_bytes=VMEM_LIMIT
        ),
    )(thermal_scalars, conductive_number, *arrays)
    return result * (2.0 / (N * N))


def solution(mesh):
    return jax.shard_map(
        per_device,
        mesh=mesh,
        in_specs=(P(None, "wall", "row", None), P(None, "wall")),
        out_specs=P(None, "wall", "row", None),
        check_vma=False,
    )
```

time: 56.3 us -> 52.8 us (0.938)
  Pallas kernels: 54.3 us -> 51.1 us
  other arithmetic: 1.88 us -> 0.83 us
  local copies, waits for them, and re-layouts: 0 us -> 0.68 us
    pallas_call x1, Pallas kernels: 54.3 us -> 51.1 us  [per_device(): pl.pallas_call(kernel, out_shape=jax.ShapeDtypeStruct(thermal_scalars.sha...]
    mul x1, other arithmetic: 1.88 us -> 0.83 us  [per_device(): return result * (2.0 / (N * N))]
    unnamed x0 -> x2, local copies, waits for them, and re-layouts: none -> 0.68 us
where the time goes in v2:
time: 52.8 us; the launch traced here: 52.6 us
  Pallas kernels  51.1 us (97%)
  other arithmetic  0.83 us (2%)
  local copies, waits for them, and re-layouts  0.68 us (1%)
    pallas_call x1, Pallas kernels, per_device(): pl.pallas_call(kernel, out_shape=jax.ShapeDtypeStruct(thermal_scalars.sha...  51.1 us

profile of v2, /device:TPU:1, one launch (start us, length us, event | category | flops | bytes accessed | tf_op | source)
XLA Modules:
  0.0 52.6 jit_solution(17698563588672429457)
XLA Ops:
  0.0 0.0 copy-start
  0.0 0.7 %copy-done = f32[2,4]{1,0:T(2,128)S(1)} copy-done((f32[2,4]{1,0:T(2,128)S(1)}, f32[2,4]{1,0:T(2,128)}, u32[]{:S(2)}) %copy-start) | copy-done | bytes 56
  0.7 51.1 %shard_map.46 = f32[2,4,16,1024]{3,2,1,0:T(8,128)S(1)} custom-call(f32[2,4,16,1024]{3,2,1,0:T(8,128)} %x_hbm.1, f32[2,4]{1,0:T(2,128)S(1)} %copy-done, bf16[2,4,128,256]{3,2,1,0:T(8,128)(2,1)} %constant.6.clone.yf_hbm, bf16[2,1664,256]{2,1,0:T(8,128)(2,1)} %constant.7.clone.tables_hbm), custom_call_target="tpu_custom_call" | custom-call | tf_op jit(solution)/shard_map/pallas_call | solution.py:416
  51.8 0.8 %broadcast_multiply_fusion = f32[2,4,16,1024]{3,2,1,0:T(8,128)} fusion(f32[2,4,16,1024]{3,2,1,0:T(8,128)S(1)} %shard_map.46), kind=kLoop, calls=%fused_computation | loop fusion | flops 131072 | bytes 1048576 | tf_op jit(solution)/shard_map/mul | solution.py:433
Async XLA Ops:
  0.0 0.7 %copy-start = (f32[2,4]{1,0:T(2,128)S(1)}, f32[2,4]{1,0:T(2,128)}, u32[]{:S(2)}) copy-start(f32[2,4]{1,0:T(2,128)} %rate_ref.1) | copy-start | bytes 100

commit v3 on v2

--- a/solution.py
+++ b/solution.py
@@ -240,6 +240,9 @@
     def near_peer(i):
         return (x // 2 * 2 + (x + i // 8) % 2) * 8 + (z + i) % 8
 
+    def farthest(t):
+        return (4 + (t + 1) // 2 * (1 - 2 * (t % 2))) % 8
+
     barrier = pltpu.get_barrier_semaphore()
 
     def greet(to):
@@ -276,9 +279,9 @@
         if h:
             pltpu.make_async_copy(src.at[xs, column], dst.at[xs, column], recv_sem.at[k]).start()
 
-        @pl.loop(h, 8)
-        def _(i):
-            c = column_peer(h, i)
+        @pl.loop(0, 8 - h)
+        def _(t):
+            c = column_peer(h, 7 - t if h else t)
             remote(src.at[xs, c], dst.at[xs, column], k, column_id(c))
 
     def expect(src, dst, k, rows, columns, out_rows, out_columns):
@@ -286,14 +289,25 @@
         return await_block(src, dst, recv_sem.at[k], rows, columns)
 
     def far_first(src, mid, k, q):
-        for h in range(2):
-            to_column(src, mid, k + q, quarter_x[q], h)
+        xs = quarter_x[q]
+        pltpu.make_async_copy(src.at[xs, column], mid.at[xs, column], recv_sem.at[k + q]).start()
+
+        def send(t, other):
+            c = (y + farthest(t)) % 8 * 2 + (core + other) % 2
+            remote(src.at[xs, c], mid.at[xs, column], k + q, column_id(c))
+
+        @pl.loop(0, 7)
+        def _(t):
+            send(t, 0)
+            send(t, 1)
+
+        send(7, 1)
         return expect(src, mid, k + q, 8, 16, 8, 15)
 
     def far_second(mid, dst, k, q):
         @pl.loop(0, 8)
         def _(i):
-            p = far_peer(q, i)
+            p = far_peer(q, farthest(i))
             remote(mid.at[p], dst.at[plane], k + 2, plane_id(p))
 
         return expect(mid, dst, k + 2, 16, 16, 16, 16) if q else None
@@ -304,10 +318,16 @@
             src.at[plane, ys], mid.at[plane, ys], recv_sem.at[k + 3 + q]
         ).start()
 
-        @pl.loop(1, 16)
-        def _(i):
+        def send(i):
             p = near_peer(i)
             remote(src.at[p, ys], mid.at[plane, ys], k + 3 + q, plane_id(p))
+
+        @pl.loop(0, 7)
+        def _(t):
+            send(8 + farthest(t))
+            send(farthest(t))
+
+        send(8)
 
         return expect(src, mid, k + 3 + q, 16, 8, 15, 8)
 
@@ -317,9 +337,9 @@
 
     zone = lax.broadcasted_iota(jnp.int32, (8, 128), 1) // 32
     for s in range(2):
-        value = jnp.full((8, 128), rate_ref[s, 0], jnp.float32)
+        value = jnp.broadcast_to(rate_ref[s : s + 1, 0:1], (8, 128))
         for j in range(1, 4):
-            value = jnp.where(zone == j, rate_ref[s, j], value)
+            value = jnp.where(zone == j, rate_ref[s : s + 1, j : j + 1], value)
         rates[wall, s] = value
     for s in range(2):
         if s == 0:
@@ -332,8 +352,9 @@
     first_steps = []
     for s in both:
         for q in both:
+            near = near_first(sent.at[s], middle.at[s], 6 * s, q)
             first_steps.append(far_first(sent.at[s], middle.at[s], 6 * s, q))
-            first_steps.append(near_first(sent.at[s], middle.at[s], 6 * s, q))
+            first_steps.append(near)
 
     @pl.loop(1, WALLS)
     def _(i):
@@ -345,10 +366,10 @@
 
     def second_steps(waits, mid, dst, k):
         for q in both:
+            waits[2 * q + 1]()
+            near = near_second(mid, dst, k, q)
             waits[2 * q]()
             far = far_second(mid, dst, k, q)
-            waits[2 * q + 1]()
-            near = near_second(mid, dst, k, q)
         return far, near
 
     arrived = [
@@ -416,7 +437,7 @@
     result = pl.pallas_call(
         kernel,
         out_shape=jax.ShapeDtypeStruct(thermal_scalars.shape, jnp.float32),
-        in_specs=[far, pl.BlockSpec(memory_space=pltpu.SMEM)] + [far] * 2,
+        in_specs=[far, pl.BlockSpec(memory_space=pltpu.VMEM), far, far],
         out_specs=pl.BlockSpec(memory_space=pltpu.VMEM),
         scratch_shapes=[
             *loaded, pltpu.VMEM((2, 64, 128), jnp.float32),

time: 52.8 us -> 50.9 us (0.964)
  Pallas kernels: 51.1 us -> 49.3 us
    pallas_call x1, Pallas kernels: 51.1 us -> 49.3 us  [per_device(): pl.pallas_call(kernel, out_shape=jax.ShapeDtypeStruct(thermal_scalars.sha...]
where the time goes in v3:
time: 50.9 us; the launch traced here: 50.8 us
  Pallas kernels  49.3 us (97%)
  other arithmetic  0.83 us (2%)
  local copies, waits for them, and re-layouts  0.68 us (1%)
    pallas_call x1, Pallas kernels, per_device(): pl.pallas_call(kernel, out_shape=jax.ShapeDtypeStruct(thermal_scalars.sha...  49.3 us

profile of v3, /device:TPU:1, one launch (start us, length us, event | category | flops | bytes accessed | tf_op | source)
XLA Modules:
  0.0 50.8 jit_solution(238608490102127303)
XLA Ops:
  0.0 0.0 copy-start
  0.0 0.7 %copy-done = f32[2,4]{1,0:T(2,128)S(1)} copy-done((f32[2,4]{1,0:T(2,128)S(1)}, f32[2,4]{1,0:T(2,128)}, u32[]{:S(2)}) %copy-start) | copy-done | bytes 56
  0.7 49.3 %shard_map.46 = f32[2,4,16,1024]{3,2,1,0:T(8,128)S(1)} custom-call(f32[2,4,16,1024]{3,2,1,0:T(8,128)} %x_hbm.1, f32[2,4]{1,0:T(2,128)S(1)} %copy-done, bf16[2,4,128,256]{3,2,1,0:T(8,128)(2,1)} %constant.6.clone.yf_hbm, bf16[2,1664,256]{2,1,0:T(8,128)(2,1)} %constant.7.clone.tables_hbm), custom_call_target="tpu_custom_call" | custom-call | tf_op jit(solution)/shard_map/pallas_call | solution.py:437
  49.9 0.8 %broadcast_multiply_fusion = f32[2,4,16,1024]{3,2,1,0:T(8,128)} fusion(f32[2,4,16,1024]{3,2,1,0:T(8,128)S(1)} %shard_map.46), kind=kLoop, calls=%fused_computation | loop fusion | flops 131072 | bytes 1048576 | tf_op jit(solution)/shard_map/mul | solution.py:454
Async XLA Ops:
  0.0 0.7 %copy-start = (f32[2,4]{1,0:T(2,128)S(1)}, f32[2,4]{1,0:T(2,128)}, u32[]{:S(2)}) copy-start(f32[2,4]{1,0:T(2,128)} %rate_ref.1) | copy-start | bytes 100

commit v4 on v3

--- a/solution.py
+++ b/solution.py
@@ -206,7 +206,7 @@
 
 def kernel(
     x_hbm, rate_ref, yf_hbm, tables_hbm, out_ref, x_ref, yf, tables, plain,
-    sent, middle, lines, spectrum, damped, damping, rates,
+    sent, middle, lines, spectrum, damped, damping, rates, numbers,
     returned, middle_back, waves, load_sem, send_sem, recv_sem, rate_sem,
 ):
     wall, row = lax.axis_index("wall"), lax.axis_index("row")
@@ -251,11 +251,11 @@
     for q in range(2):
         for i in (4, 3, 5, 2, 6, 1, 7, 0):
             greet(plane_id(far_peer(q, i)))
+    for i in (12, 11, 13, 4, 10, 14, 3, 5, 9, 15, 2, 6, 8, 1, 7):
+        greet(plane_id(near_peer(i)))
     for i in range(8):
         greet(column_id(column_peer(0, i)))
-    for i in range(15, 0, -1):
-        greet(plane_id(near_peer(i)))
-    for i in range(1, 8):
+    for i in range(7, 0, -1):
         greet(column_id(column_peer(1, i)))
 
     loads[3].start()
@@ -335,12 +335,11 @@
         to_column(mid, dst, k + 5, half_x[1], q)
         return expect(mid, dst, k + 5, 16, 16, 16, 15) if q else None
 
-    zone = lax.broadcasted_iota(jnp.int32, (8, 128), 1) // 32
-    for s in range(2):
-        value = jnp.broadcast_to(rate_ref[s : s + 1, 0:1], (8, 128))
-        for j in range(1, 4):
-            value = jnp.where(zone == j, rate_ref[s : s + 1, j : j + 1], value)
-        rates[wall, s] = value
+    zone = lax.broadcasted_iota(jnp.int32, (2, 128), 1) // 32
+    value = jnp.broadcast_to(rate_ref[:, 0:1], (2, 128))
+    for j in range(1, 4):
+        value = jnp.where(zone == j, rate_ref[:, j : j + 1], value)
+    numbers[wall] = value
     for s in range(2):
         if s == 0:
             loads[1].wait()
@@ -359,7 +358,7 @@
     @pl.loop(1, WALLS)
     def _(i):
         pltpu.make_async_remote_copy(
-            src_ref=rates.at[wall], dst_ref=rates.at[wall],
+            src_ref=numbers.at[wall], dst_ref=numbers.at[wall],
             send_sem=rate_sem.at[0], recv_sem=rate_sem.at[1],
             device_id=(lax.rem(wall + i, WALLS), row), device_id_type=MESH,
         ).start()
@@ -378,7 +377,10 @@
     ]
 
     group = pl.ds(0, WALLS - 1)
-    pltpu.make_async_copy(rates.at[group], rates.at[group], rate_sem.at[1]).wait()
+    pltpu.make_async_copy(numbers.at[group], numbers.at[group], rate_sem.at[1]).wait()
+    for w in range(WALLS):
+        for s in both:
+            rates[w, s] = jnp.broadcast_to(numbers[w, s : s + 1], (8, 128))
     loads[3].wait()
     for j in range(2):
         terms = [tables[(j, *turn_place(i))].astype(jnp.float32) for i in range(3)]
@@ -406,7 +408,7 @@
 
     first_steps = []
     for s in both:
-        for h in both:
+        for h in (1, 0):
             arrived[s][h]()
             for w in slabs[h]:
                 to_spectrum(lines, tables, plain, spectrum, s, w)
@@ -423,7 +425,7 @@
         for wait in arrived[s]:
             wait()
         from_waves(waves, tables, out_ref, s)
-    pltpu.make_async_copy(rates.at[group], rates.at[group], rate_sem.at[0]).wait()
+    pltpu.make_async_copy(numbers.at[group], numbers.at[group], rate_sem.at[0]).wait()
     for wait in done:
         wait()
 
@@ -442,7 +444,7 @@
         scratch_shapes=[
             *loaded, pltpu.VMEM((2, 64, 128), jnp.float32),
             block, block, block, cube, pltpu.VMEM((WALLS, 64, 128), jnp.float32), cube,
-            pltpu.VMEM((WALLS, 2, 8, 128), jnp.float32),
+            pltpu.VMEM((WALLS, 2, 8, 128), jnp.float32), pltpu.VMEM((WALLS, 2, 128), jnp.float32),
             block, block, block,
             pltpu.SemaphoreType.DMA((4,)), pltpu.SemaphoreType.DMA((24,)),
             pltpu.SemaphoreType.DMA((24,)), pltpu.SemaphoreType.DMA((2,)),

time: 50.9 us -> 49.9 us (0.980)
  Pallas kernels: 49.3 us -> 48.2 us
    pallas_call x1, Pallas kernels: 49.3 us -> 48.2 us  [per_device(): pl.pallas_call(kernel, out_shape=jax.ShapeDtypeStruct(thermal_scalars.sha...]
where the time goes in v4:
time: 49.9 us; the launch traced here: 49.7 us
  Pallas kernels  48.2 us (97%)
  other arithmetic  0.83 us (2%)
  local copies, waits for them, and re-layouts  0.68 us (1%)
    pallas_call x1, Pallas kernels, per_device(): pl.pallas_call(kernel, out_shape=jax.ShapeDtypeStruct(thermal_scalars.sha...  48.2 us

profile of v4, /device:TPU:1, one launch (start us, length us, event | category | flops | bytes accessed | tf_op | source)
XLA Modules:
  0.0 49.7 jit_solution(17638667256519463229)
XLA Ops:
  0.0 0.0 copy-start
  0.0 0.7 %copy-done = f32[2,4]{1,0:T(2,128)S(1)} copy-done((f32[2,4]{1,0:T(2,128)S(1)}, f32[2,4]{1,0:T(2,128)}, u32[]{:S(2)}) %copy-start) | copy-done | bytes 56
  0.7 48.2 %shard_map.46 = f32[2,4,16,1024]{3,2,1,0:T(8,128)S(1)} custom-call(f32[2,4,16,1024]{3,2,1,0:T(8,128)} %x_hbm.1, f32[2,4]{1,0:T(2,128)S(1)} %copy-done, bf16[2,4,128,256]{3,2,1,0:T(8,128)(2,1)} %constant.6.clone.yf_hbm, bf16[2,1664,256]{2,1,0:T(8,128)(2,1)} %constant.7.clone.tables_hbm), custom_call_target="tpu_custom_call" | custom-call | tf_op jit(solution)/shard_map/pallas_call | solution.py:439
  48.9 0.8 %broadcast_multiply_fusion = f32[2,4,16,1024]{3,2,1,0:T(8,128)} fusion(f32[2,4,16,1024]{3,2,1,0:T(8,128)S(1)} %shard_map.46), kind=kLoop, calls=%fused_computation | loop fusion | flops 131072 | bytes 1048576 | tf_op jit(solution)/shard_map/mul | solution.py:456
Async XLA Ops:
  0.0 0.7 %copy-start = (f32[2,4]{1,0:T(2,128)S(1)}, f32[2,4]{1,0:T(2,128)}, u32[]{:S(2)}) copy-start(f32[2,4]{1,0:T(2,128)} %rate_ref.1) | copy-start | bytes 100

commit v5 on v4

--- a/solution.py
+++ b/solution.py
@@ -331,6 +331,37 @@
 
         return expect(src, mid, k + 3 + q, 16, 8, 15, 8)
 
+    def both_first(src, mid, k, q):
+        xs, ys = quarter_x[q], half_y[q]
+        local = [
+            (src.at[plane, ys], mid.at[plane, ys], k + 3 + q),
+            (src.at[xs, column], mid.at[xs, column], k + q),
+        ]
+        for here, there, sem in local:
+            pltpu.make_async_copy(here, there, recv_sem.at[sem]).start()
+
+        def near(i):
+            p = near_peer(i)
+            remote(src.at[p, ys], mid.at[plane, ys], k + 3 + q, plane_id(p))
+
+        def far(t, other):
+            c = (y + farthest(t)) % 8 * 2 + (core + other) % 2
+            remote(src.at[xs, c], mid.at[xs, column], k + q, column_id(c))
+
+        @pl.loop(0, 7)
+        def _(t):
+            near(8 + farthest(t))
+            far(t, 0)
+            near(farthest(t))
+            far(t, 1)
+
+        near(8)
+        far(7, 1)
+        return [
+            expect(src, mid, k + q, 8, 16, 8, 15),
+            expect(src, mid, k + 3 + q, 16, 8, 15, 8),
+        ]
+
     def near_second(mid, dst, k, q):
         to_column(mid, dst, k + 5, half_x[1], q)
         return expect(mid, dst, k + 5, 16, 16, 16, 15) if q else None
@@ -351,9 +382,7 @@
     first_steps = []
     for s in both:
         for q in both:
-            near = near_first(sent.at[s], middle.at[s], 6 * s, q)
-            first_steps.append(far_first(sent.at[s], middle.at[s], 6 * s, q))
-            first_steps.append(near)
+            first_steps += both_first(sent.at[s], middle.at[s], 6 * s, q)
 
     @pl.loop(1, WALLS)
     def _(i):

time: 49.9 us -> 49.1 us (0.984)
  Pallas kernels: 48.2 us -> 47.4 us
    pallas_call x1, Pallas kernels: 48.2 us -> 47.4 us  [per_device(): pl.pallas_call(kernel, out_shape=jax.ShapeDtypeStruct(thermal_scalars.sha...]
where the time goes in v5:
time: 49.1 us; the launch traced here: 48.9 us
  Pallas kernels  47.4 us (97%)
  other arithmetic  0.83 us (2%)
  local copies, waits for them, and re-layouts  0.68 us (1%)
    pallas_call x1, Pallas kernels, per_device(): pl.pallas_call(kernel, out_shape=jax.ShapeDtypeStruct(thermal_scalars.sha...  47.4 us

profile of v5, /device:TPU:1, one launch (start us, length us, event | category | flops | bytes accessed | tf_op | source)
XLA Modules:
  0.0 48.9 jit_solution(17212580714381601882)
XLA Ops:
  0.0 0.0 copy-start
  0.0 0.7 %copy-done = f32[2,4]{1,0:T(2,128)S(1)} copy-done((f32[2,4]{1,0:T(2,128)S(1)}, f32[2,4]{1,0:T(2,128)}, u32[]{:S(2)}) %copy-start) | copy-done | bytes 56
  0.7 47.4 %shard_map.46 = f32[2,4,16,1024]{3,2,1,0:T(8,128)S(1)} custom-call(f32[2,4,16,1024]{3,2,1,0:T(8,128)} %x_hbm.1, f32[2,4]{1,0:T(2,128)S(1)} %copy-done, bf16[2,4,128,256]{3,2,1,0:T(8,128)(2,1)} %constant.6.clone.yf_hbm, bf16[2,1664,256]{2,1,0:T(8,128)(2,1)} %constant.7.clone.tables_hbm), custom_call_target="tpu_custom_call" | custom-call | tf_op jit(solution)/shard_map/pallas_call | solution.py:468
  48.1 0.8 %broadcast_multiply_fusion = f32[2,4,16,1024]{3,2,1,0:T(8,128)} fusion(f32[2,4,16,1024]{3,2,1,0:T(8,128)S(1)} %shard_map.46), kind=kLoop, calls=%fused_computation | loop fusion | flops 131072 | bytes 1048576 | tf_op jit(solution)/shard_map/mul | solution.py:485
Async XLA Ops:
  0.0 0.7 %copy-start = (f32[2,4]{1,0:T(2,128)S(1)}, f32[2,4]{1,0:T(2,128)}, u32[]{:S(2)}) copy-start(f32[2,4]{1,0:T(2,128)} %rate_ref.1) | copy-start | bytes 100
